TPU v7x, 32 devices: a whole 2x2x4 slice. The times are simulated.
32 devices in a mesh: ctx: 8 (over y, x, core), hs: 4 (over z).
Axes of the slice: x: 2, y: 2, z: 4, core: 2. Of those that a mesh axis runs over, the one named last changes fastest.
Arguments:
- queries: bfloat16 [4, 8192, 512], P('hs', 'ctx'), may hold values from -40 to 40
- keys: bfloat16 [4, 8192, 512], P('hs', 'ctx'), may hold values from -6 to 6
- values: bfloat16 [4, 8192, 512], P('hs', 'ctx'), may hold values from -6 to 6
- rates: float32 [4, 8192], P('hs', 'ctx'), may hold values from 0.02 to 0.2
- doc_ids: int32 [2, 8192], replicated, may hold values from 0 to 3, never falling along the last dimension, each value on 1 to 4096 neighbouring positions
- fast_weights: bfloat16 [4, 3, 512, 512], P('hs'), may hold values from -0.25 to 0.25
- momentum: float32 [4, 3, 512, 512], P('hs'), may hold values from -0.2 to 0.2
- head_gain: float32 [4, 512], P('hs'), may hold values from 0.5 to 2
Outputs:
- tokens_out: bfloat16 [4, 8192, 512], P('hs', 'ctx')
- new_weights: bfloat16 [4, 3, 512, 512], P('hs')
Inputs may be any that keep to these rules, and one draw needn't show every extreme that they name: `doc_ids`: each row never falls; a document has at most 4096 positions and some document has exactly that many.
All inputs are finite; a program needn't handle non-finite values.
Results may differ from a plain program's by a relative error of at most 0.0092.
Values may be sent and summed in bfloat16 or wider, within the bound.
A program may use at most 64 MiB of HBM per device.

v0:
```python
import functools
import math

import jax
import jax.numpy as jnp
from jax import lax
from jax.experimental import pallas as pl
from jax.experimental.pallas import tpu as pltpu
from jax.sharding import PartitionSpec as P

WINDOW_TOKENS = 512
BLOCK = 256
MESH = pl.DeviceIdType.MESH
F32 = jnp.float32
PLAN = "fBghPQ201E201VE201201HL2012L"
BF16 = jnp.bfloat16


def as_column(row):
    return jnp.transpose(jnp.broadcast_to(row, (128, row.shape[1])), (1, 0))


def kernel(
    n, heads, seqs,
    q_hbm, k_hbm, v_hbm, rates_ref, doc_ref, w_hbm, mom_hbm, gain_ref,
    out_hbm, new_hbm,
    q, kx, vx, w, mom, dh, u, acc, sbuf, rbuf, cand, base, old_rms, hold, y, outbuf,
    ss_own, ss_got, doc_cols,
    local_sem, halo_send, halo_recv, rs_send, rs_recv, ag_send, ag_recv, ss_send, ss_recv, out_sem,
):
    rows, width = q.shape
    win = WINDOW_TOKENS
    wrows = w.shape[1]
    phases = n.bit_length() - 1
    blocks = rows // BLOCK
    me = lax.axis_index("ctx")
    hs = lax.axis_index("hs")
    seq = hs // heads
    head_base = seq * heads
    peers = [head_base + (hs - head_base + d) % heads for d in range(1, heads)]

    bits = [(me // (1 << i)) % 2 for i in range(phases)]
    core = bits[0]
    forward = list(range(phases))
    other = [0] + list(range(phases - 1, 0, -1))
    partner, keep, drop = [], [], []
    low = 0
    for j in range(phases):
        a, b = forward[j], other[j]
        bit = bits[a] if a == b else bits[a] * (1 - core) + bits[b] * core
        stride = (1 << a) if a == b else (1 << a) * (1 - core) + (1 << b) * core
        half = wrows >> (j + 1)
        partner.append(me + (1 - 2 * bit) * stride)
        keep.append(low + bit * half)
        drop.append(low + (1 - bit) * half)
        low = low + bit * half
    own = wrows >> phases

    def at_rows(start, size):
        return pl.ds(pl.multiple_of(start, size), size)

    lane_block = (low // 128) * 128
    lanes_own = pl.ds(pl.multiple_of(lane_block, 128), 128)
    within = at_rows(low - lane_block, own)
    loads = [
        pltpu.make_async_copy(k_hbm, kx.at[pl.ds(win, rows)], local_sem.at[0]),
        pltpu.make_async_copy(w_hbm, w, local_sem.at[1]),
        pltpu.make_async_copy(v_hbm, vx.at[pl.ds(win, rows)], local_sem.at[2]),
        pltpu.make_async_copy(q_hbm, q, local_sem.at[3]),
        pltpu.make_async_copy(mom_hbm.at[:, :, lanes_own], mom, local_sem.at[4]),
    ]
    for load in loads:
        load.start()

    barrier = pltpu.get_barrier_semaphore()
    for d in range(1, n):
        pl.semaphore_signal(barrier, 1, device_id={"ctx": (me + d) % n}, device_id_type=MESH)
    for peer in peers:
        pl.semaphore_signal(barrier, 1, device_id={"hs": peer}, device_id_type=MESH)
    pl.semaphore_wait(barrier, n - 1 + len(peers))

    halo = [
        pltpu.make_async_remote_copy(
            src_ref=src.at[pl.ds(rows - win, win)], dst_ref=dst.at[pl.ds(0, win)],
            send_sem=halo_send.at[i], recv_sem=halo_recv.at[i],
            device_id={"ctx": (me + 1) % n}, device_id_type=MESH,
        )
        for i, (src, dst) in enumerate(((k_hbm, kx), (v_hbm, vx)))
    ]

    def halo_start(i):
        @pl.when(me < n - 1)
        def _():
            halo[i].start()

    halo_start(0)
    if "V" not in PLAN:
        halo_start(1)

    @pl.when(me == 0)
    def _():
        kx[0:win, :] = jnp.zeros((win, width), BF16)
        vx[0:win, :] = jnp.zeros((win, width), BF16)

    offset = me * rows
    before = jnp.maximum(me * rows - win, 0)
    docs = jnp.concatenate(
        [doc_ref[:, pl.ds(pl.multiple_of(before, 128), win)],
         doc_ref[:, pl.ds(pl.multiple_of(offset, 128), rows)]], axis=1)
    pick = lax.broadcasted_iota(jnp.int32, docs.shape, 0) == seq
    doc_row = jnp.sum(jnp.where(pick, docs, 0), axis=0, keepdims=True).astype(F32)
    doc_cols[...] = as_column(doc_row[:, win:])
    rate_cols = as_column(rates_ref[...])

    loads[0].wait()
    loads[1].wait()
    loads[2].wait()
    total = rows * n
    for i in range(blocks):
        at = pl.ds(i * BLOCK, BLOCK)
        kb = kx[pl.ds(win + i * BLOCK, BLOCK), :]
        vb = vx[pl.ds(win + i * BLOCK, BLOCK), :].astype(F32)
        rate = rate_cols[i * BLOCK:(i + 1) * BLOCK, :1]
        u[at, :] = (rate * vb * (-1.0 / math.sqrt(total))).astype(BF16)
        h1 = jnp.dot(kb, w[0], preferred_element_type=F32)
        h3 = jnp.dot(kb, w[1], preferred_element_type=F32)
        sig = 1.0 / (1.0 + jnp.exp(-h1))
        act = h1 * sig
        dh[2, at, :] = (act * h3).astype(BF16)
        hold[0, at, :] = h3 * sig * (1.0 + h1 * (1.0 - sig))
        hold[1, at, :] = act

    def slot(j):
        return pl.ds(wrows - (wrows >> j), wrows >> (j + 1))

    def scatter(c, j):
        return pltpu.make_async_remote_copy(
            src_ref=sbuf.at[c, slot(j), :], dst_ref=rbuf.at[c, slot(j), :],
            send_sem=rs_send.at[c, j], recv_sem=rs_recv.at[c, j],
            device_id={"ctx": partner[j]}, device_id_type=MESH)

    def scatter_start(c, j):
        half = wrows >> (j + 1)
        sbuf[c, slot(j), :] = acc[c, at_rows(drop[j], half), :].astype(BF16)
        scatter(c, j).start()

    def scatter_finish(c, j):
        half = wrows >> (j + 1)
        scatter(c, j).wait_recv()
        mine = at_rows(keep[j], half)
        acc[c, mine, :] = acc[c, mine, :] + rbuf[c, slot(j), :].astype(F32)

    def gather(c, j):
        mine = at_rows(keep[j], wrows >> (j + 1))
        return pltpu.make_async_remote_copy(
            src_ref=cand.at[c, mine, :], dst_ref=cand.at[c, mine, :],
            send_sem=ag_send.at[c, j], recv_sem=ag_recv.at[c, j],
            device_id={"ctx": partner[j]}, device_id_type=MESH)

    def gather_wait(c, j):
        theirs = at_rows(drop[j], wrows >> (j + 1))
        pltpu.make_async_remote_copy(
            src_ref=cand.at[c, theirs, :], dst_ref=cand.at[c, theirs, :],
            send_sem=ag_send.at[c, j], recv_sem=ag_recv.at[c, j],
            device_id={"ctx": partner[j]}, device_id_type=MESH).wait_recv()

    def attend(i):
        at = pl.ds(i * BLOCK, BLOCK)
        span = win + BLOCK
        kb = kx[pl.ds(i * BLOCK, span), :]
        scores = lax.dot_general(
            q[at, :], kb, (((1,), (1,)), ((), ())), preferred_element_type=F32
        ) * (1.0 / math.sqrt(width))
        qpos = lax.broadcasted_iota(jnp.int32, scores.shape, 0) + win
        kpos = lax.broadcasted_iota(jnp.int32, scores.shape, 1)
        first = win - offset - i * BLOCK
        valid = (
            (kpos <= qpos) & (kpos > qpos - win) & (kpos >= first)
            & (doc_row[:, i * BLOCK:i * BLOCK + span] == doc_cols[at, :][:, :1])
        )
        scores = jnp.where(valid, scores, -1e30)
        top = jnp.max(scores, axis=1, keepdims=True)
        expo = jnp.exp(scores - top)
        norm = 1.0 / jnp.sum(expo, axis=1, keepdims=True)
        y[at, :] = jnp.dot(
            expo.astype(BF16), vx[pl.ds(i * BLOCK, span), :], preferred_element_type=F32) * norm

    def halo_wait():
        @pl.when(me > 0)
        def _():
            halo[0].wait_recv()
            halo[1].wait_recv()

    def prepare():
        loads[4].wait()
        for c in range(3):
            old = jnp.transpose(w[c, :, lanes_own].astype(F32), (1, 0))
            base[c] = old - 0.9 * jnp.transpose(mom[c], (1, 0))
            rms = jnp.sqrt(jnp.mean(old * old, axis=1, keepdims=True) + 1e-06)
            old_rms[c] = jnp.broadcast_to(rms, old_rms.shape[1:])

    def renew(c):
        mine = at_rows(low, own)
        part = base[c, within, :] - acc[c, mine, :]
        ratio = old_rms[c, within, :][:, :1] * lax.rsqrt(
            jnp.mean(part * part, axis=1, keepdims=True) + 1e-06)
        cand[c, mine, :] = (part * ratio).astype(BF16)

    taken = [0, 0, 0]

    def advance(c):
        step = taken[c]
        if step == 2 * phases:
            return
        taken[c] += 1
        if step < phases:
            scatter_finish(c, step)
            if step + 1 < phases:
                scatter_start(c, step + 1)
            else:
                renew(c)
                gather(c, phases - 1).start()
        else:
            j = 2 * phases - 1 - step
            gather_wait(c, j)
            if j > 0:
                gather(c, j - 1).start()
            else:
                pltpu.make_async_copy(cand.at[c], new_hbm.at[c], out_sem.at[c]).start()

    across = (((0,), (0,)), ((), ()))
    nt = (((1,), (1,)), ((), ()))

    def gradient(c):
        right = u[...] if c == 2 else kx[pl.ds(win, rows), :]
        acc[c] = lax.dot_general(dh[c], right, across, preferred_element_type=F32)
        scatter_start(c, 0)

    def back():
        for i in range(blocks):
            at = pl.ds(i * BLOCK, BLOCK)
            dg = jnp.dot(u[at, :], w[2], preferred_element_type=F32)
            dh[0, at, :] = (dg * hold[0, at, :]).astype(BF16)
            dh[1, at, :] = (dg * hold[1, at, :]).astype(BF16)

    early = [i for i in range(blocks) if i * BLOCK >= win]
    late = [i for i in range(blocks) if i * BLOCK < win]
    steps = {
        "B": back, "P": prepare, "H": halo_wait, "Q": loads[3].wait,
        "V": lambda: halo_start(1),
        "E": lambda: attend(early.pop(0)), "L": lambda: attend(late.pop(0)),
        "g": lambda: gradient(0), "h": lambda: gradient(1), "f": lambda: gradient(2),
        "0": lambda: advance(0), "1": lambda: advance(1), "2": lambda: advance(2),
    }
    for step in PLAN:
        steps[step]()
    while taken[0] < 2 * phases:
        for c in range(3):
            if taken[c] < 2 * phases - (1 if c else 0):
                advance(c)
    for i in range(blocks):
        at = pl.ds(i * BLOCK, BLOCK)
        o1 = lax.dot_general(q[at, :], cand[0], nt, preferred_element_type=F32)
        hold[0, at, :] = o1 / (1.0 + jnp.exp(-o1))
    while taken[1] < 2 * phases:
        advance(1)
    if taken[2] < 2 * phases - 1:
        advance(2)
    for i in range(blocks):
        at = pl.ds(i * BLOCK, BLOCK)
        o3 = lax.dot_general(q[at, :], cand[1], nt, preferred_element_type=F32)
        u[at, :] = (hold[0, at, :] * o3).astype(BF16)
    while taken[2] < 2 * phases:
        advance(2)

    def squares_copy(d, i):
        return pltpu.make_async_remote_copy(
            src_ref=ss_own.at[i], dst_ref=ss_got.at[d, i],
            send_sem=ss_send.at[d, i], recv_sem=ss_recv.at[d, i],
            device_id={"hs": peers[d]}, device_id_type=MESH)

    for i in range(blocks):
        at = pl.ds(i * BLOCK, BLOCK)
        mixed = y[at, :] + jnp.dot(u[at, :], cand[2], preferred_element_type=F32)
        y[at, :] = mixed
        sq = mixed * mixed
        lanes = sq[:, 0:128]
        for s in range(1, width // 128):
            lanes = lanes + sq[:, s * 128:(s + 1) * 128]
        row = jnp.sum(jnp.transpose(lanes, (1, 0)), axis=0, keepdims=True)
        ss_own[i] = jnp.broadcast_to(row, ss_own.shape[1:])
        for d in range(len(peers)):
            squares_copy(d, i).start()

    for i in range(blocks):
        at = pl.ds(i * BLOCK, BLOCK)
        row = ss_own[i][0:1, :]
        for d in range(len(peers)):
            squares_copy(d, i).wait_recv()
            row = row + ss_got[d, i][0:1, :]
        scale = lax.rsqrt(as_column(row) * (1.0 / (heads * width)) + 1e-06)
        gain = gain_ref[...]
        for s in range(width // 128):
            cols = slice(s * 128, (s + 1) * 128)
            outbuf[at, cols] = (y[at, cols] * scale * gain[:, cols]).astype(BF16)
        pltpu.make_async_copy(outbuf.at[at], out_hbm.at[at], out_sem.at[3 + i]).start()

    for c in range(3):
        for j in range(phases):
            scatter(c, j).wait_send()
            gather(c, j).wait_send()
        pltpu.make_async_copy(cand.at[c], new_hbm.at[c], out_sem.at[c]).wait()
    for i in range(blocks):
        at = pl.ds(i * BLOCK, BLOCK)
        for d in range(len(peers)):
            squares_copy(d, i).wait_send()
        pltpu.make_async_copy(outbuf.at[at], out_hbm.at[at], out_sem.at[3 + i]).wait()

    @pl.when(me < n - 1)
    def _():
        halo[0].wait_send()
        halo[1].wait_send()


def per_device(n, hs_count, queries, keys, values, rates, doc_ids, fast_weights, momentum, head_gain):
    rows, width = queries.shape[1:]
    _, mats, wrows, wcols = fast_weights.shape
    seqs = doc_ids.shape[0]
    heads = hs_count // seqs
    phases = n.bit_length() - 1
    own = wrows >> phases
    blocks = rows // BLOCK
    ext = rows + WINDOW_TOKENS
    others = max(heads - 1, 1)
    any_spec = pl.BlockSpec(memory_space=pl.ANY)
    vmem = pl.BlockSpec(memory_space=pltpu.VMEM)
    dma = pltpu.SemaphoreType.DMA
    out, fresh = pl.pallas_call(
        functools.partial(kernel, n, heads, seqs),
        out_shape=(
            jax.ShapeDtypeStruct((rows, width), BF16),
            jax.ShapeDtypeStruct((mats, wrows, wcols), BF16),
        ),
        in_specs=[any_spec, any_spec, any_spec, vmem, vmem, any_spec, any_spec, vmem],
        out_specs=(any_spec, any_spec),
        scratch_shapes=[
            pltpu.VMEM((rows, width), BF16),
            pltpu.VMEM((ext, width), BF16),
            pltpu.VMEM((ext, width), BF16),
            pltpu.VMEM((mats, wrows, wcols), BF16),
            pltpu.VMEM((mats, wrows, 128), F32),
            pltpu.VMEM((mats, rows, wcols), BF16),
            pltpu.VMEM((rows, width), BF16),
            pltpu.VMEM((mats, wrows, wcols), F32),
            pltpu.VMEM((mats, wrows, wcols), BF16),
            pltpu.VMEM((mats, wrows, wcols), BF16),
            pltpu.VMEM((mats, wrows, wcols), BF16),
            pltpu.VMEM((mats, 128, wrows), F32),
            pltpu.VMEM((mats, 128, 128), F32),
            pltpu.VMEM((2, rows, wcols), F32),
            pltpu.VMEM((rows, width), F32),
            pltpu.VMEM((rows, width), BF16),
            pltpu.VMEM((blocks, 8, BLOCK), F32),
            pltpu.VMEM((others, blocks, 8, BLOCK), F32),
            pltpu.VMEM((rows, 128), F32),
            dma((5,)), dma((2,)), dma((2,)),
            dma((3, phases)), dma((3, phases)), dma((3, phases)), dma((3, phases)),
            dma((others, blocks)), dma((others, blocks)), dma((3 + blocks,)),
        ],
        compiler_params=pltpu.CompilerParams(
            collective_id=0, has_side_effects=True, vmem_limit_bytes=60 * 1024 * 1024),
        name="lact_block",
    )(queries[0], keys[0], values[0], rates, doc_ids, fast_weights[0], momentum[0], head_gain)
    return out[None], jnp.swapaxes(fresh, 1, 2)[None]


def solution(mesh):
    return jax.shard_map(
        functools.partial(per_device, mesh.shape["ctx"], mesh.shape["hs"]),
        mesh=mesh,
        in_specs=(
            P("hs", "ctx", None),
            P("hs", "ctx", None),
            P("hs", "ctx", None),
            P("hs", "ctx"),
            P(),
            P("hs", None, None, None),
            P("hs", None, None, None),
            P("hs", None),
        ),
        out_specs=(P("hs", "ctx", None), P("hs", None, None, None)),
        check_vma=False,
    )
```

profile of v0, /device:TPU:0, one launch (start us, length us, event | category | flops | bytes accessed | tf_op | source)
XLA Modules:
  0.0 43.9 jit_solution(12559389343983534938)
XLA Ops:
  0.6 39.6 %lact_block.1 = (bf16[1024,512]{1,0:T(8,128)(2,1)}, bf16[3,512,512]{2,1,0:T(8,128)(2,1)}) custom-call(bf16[1024,512]{1,0:T(8,128)(2,1)} %bitcast.12, bf16[1024,512]{1,0:T(8,128)(2,1)} %bitcast.13, bf16[1024,512]{1,0:T(8,128)(2,1)} %bitcast.14, f32[1,1024]{1,0:T(1,128)} %rates_ref.1, s32[2,8192]{1,0:T(2,128)} %doc_ref.1, bf16[3,512,512]{2,1,0:T(8,128)(2,1)} %bitcast.11, ...), custom_call_target="tpu_custom_call" | custom-call | tf_op jit(solution)/shard_map/lact_block/pallas_call | solution.py:338
  40.2 0.0 copy-start
  40.2 2.7 %copy.10 = bf16[1,3,512,512]{3,2,1,0:T(8,128)(2,1)} copy(bf16[1,3,512,512]{2,3,1,0:T(8,128)(2,1)} %bitcast.10) | data formatting | bytes 3145728
  42.9 0.0 copy-done
  42.9 1.0 %copy.12 = bf16[1,1024,512]{2,1,0:T(8,128)(2,1)} copy(bf16[1,1024,512]{2,1,0:T(8,128)(2,1)S(1)} %bitcast.15) | data formatting | bytes 2097152
Async XLA Ops:
  40.2 2.7 %copy-start = (bf16[1024,512]{1,0:T(8,128)(2,1)S(1)}, bf16[1024,512]{1,0:T(8,128)(2,1)}, u32[]{:S(2)}) copy-start(bf16[1024,512]{1,0:T(8,128)(2,1)} %get-tuple-element.4) | copy-start | bytes 3145732
where the time goes:
time: 44.1 us; the launch traced here: 43.9 us
  Pallas kernels  39.6 us (90%)
  local copies, waits for them, and re-layouts  3.64 us (8%)
  between operations  0.65 us (1%)
    pallas_call x1, Pallas kernels, per_device(): pl.pallas_call(functools.partial(kernel, n, heads, seqs), out_shape=(jax....  39.6 us
    unnamed x4, local copies, waits for them, and re-layouts  3.64 us

commit v1 on v0

v1 whole, which is shorter than its diff:
```python
import functools
import math

import jax
import jax.numpy as jnp
from jax import lax
from jax.experimental import pallas as pl
from jax.experimental.pallas import tpu as pltpu
from jax.sharding import PartitionSpec as P

WINDOW_TOKENS = 512
BLOCK = 256
QBLOCK = 512
MESH = pl.DeviceIdType.MESH
F32 = jnp.float32
PLAN = (
    "|", "F", "F", "F", "F", "g4", "g5", "B0", "g0", "4", "g2", "B1", "5", "g1", "0", "4", "g3",
    "2", "5", "P4", "P5", "D", "Q", "0", "E", "4", "V", "1", "2", "5", "V", "3", "P0", "P2", "0",
    "V", "4", "1", "E", "2", "V", "5", "3", "P1", "P3", "K", "0", "4", "S", "1", "V", "2", "5", "3",
    "V", "4", "0", "S", "1", "V", "5", "2", "3", "V", "0", "2", "O0", "1", "M0", "r", "3", "W0",
    "1", "O1", "r", "3", "M1",
)
FIRST = ("xy", "xy", "xy", "xy", "xy", "xy",)
SPLIT = 2
PIECES = 8
BF16 = jnp.bfloat16


def as_column(row):
    return jnp.transpose(jnp.broadcast_to(row, (128, row.shape[1])), (1, 0))


def kernel(
    n, heads, seqs,
    q_hbm, k_hbm, v_hbm, rates_hbm, doc_hbm, w_hbm, mom_hbm, gain_hbm,
    y, wt, ss_out, gain_out,
    q, kx, vx, w, mom, docs, rates, dh, u, acc, sbuf, rbuf, cand, base, old_rms, hold,
    gq, held, norms, ss_own, ss_got, doc_cols,
    k_sem, v_sem, w_sem, local_sem, halo_send, halo_recv,
    rs_send, rs_recv, ag_send, ag_recv, ss_send, ss_recv,
):
    rows, width = q.shape
    win = WINDOW_TOKENS
    wrows = w.shape[1]
    phases = n.bit_length() - 1
    blocks = rows // BLOCK
    me = lax.axis_index("ctx")
    hs = lax.axis_index("hs")
    seq = hs // heads
    head_base = seq * heads
    peers = [head_base + (hs - head_base + d) % heads for d in range(1, heads)]
    offset = me * rows
    before = jnp.maximum(me * rows - win, 0)

    bits = [(me // (1 << i)) % 2 for i in range(phases)]
    core = bits[0]
    orders = {"x": list(range(phases)), "y": [0] + list(range(phases - 1, 0, -1))}
    chunks = 3 * SPLIT
    crows = wrows // SPLIT
    own = crows >> phases
    partner, keep, drop, low = [], [], [], []
    for c in range(chunks):
        mine_first, other_first = orders[FIRST[c][0]], orders[FIRST[c][1]]
        partner.append([])
        keep.append([])
        drop.append([])
        at = (c % SPLIT) * crows
        for j in range(phases):
            a, b = mine_first[j], other_first[j]
            bit = bits[a] if a == b else bits[a] * (1 - core) + bits[b] * core
            stride = (1 << a) if a == b else (1 << a) * (1 - core) + (1 << b) * core
            half = crows >> (j + 1)
            partner[c].append(me + (1 - 2 * bit) * stride)
            keep[c].append(at + bit * half)
            drop[c].append(at + (1 - bit) * half)
            at = at + bit * half
        low.append(at)

    def at_rows(start, size):
        return pl.ds(pl.multiple_of(start, size), size)

    lanes_own = [pl.ds(pl.multiple_of((at // 128) * 128, 128), 128) for at in low]
    within = [at_rows(at - (at // 128) * 128, own) for at in low]

    def block_at(i, start=0):
        return pl.ds(start + i * BLOCK, BLOCK)

    k_loads = [pltpu.make_async_copy(k_hbm.at[block_at(i)], kx.at[block_at(i, win)], k_sem.at[i])
               for i in range(blocks)]
    v_loads = [pltpu.make_async_copy(v_hbm.at[block_at(i)], vx.at[block_at(i, win)], v_sem.at[i])
               for i in range(blocks)]
    w_loads = [pltpu.make_async_copy(w_hbm.at[c], w.at[c], w_sem.at[c]) for c in range(3)]
    doc_loads = [
        pltpu.make_async_copy(
            doc_hbm.at[:, pl.ds(pl.multiple_of(before, 128), win)],
            docs.at[:, pl.ds(0, win)], local_sem.at[0]),
        pltpu.make_async_copy(
            doc_hbm.at[:, pl.ds(pl.multiple_of(offset, 128), rows)],
            docs.at[:, pl.ds(win, rows)], local_sem.at[1]),
    ]
    rate_load = pltpu.make_async_copy(rates_hbm, rates, local_sem.at[2])
    gain_load = pltpu.make_async_copy(gain_hbm, gain_out, local_sem.at[3])
    q_load = pltpu.make_async_copy(q_hbm, q, local_sem.at[4])
    mom_loads = [pltpu.make_async_copy(mom_hbm.at[c // SPLIT, :, lanes_own[c]], mom.at[c], local_sem.at[5 + c])
                 for c in range(chunks)]

    barrier = pltpu.get_barrier_semaphore()
    for d in range(1, n):
        pl.semaphore_signal(barrier, 1, device_id={"ctx": (me + d) % n}, device_id_type=MESH)
    for peer in peers:
        pl.semaphore_signal(barrier, 1, device_id={"hs": peer}, device_id_type=MESH)

    for load in [k_loads[0], w_loads[0], w_loads[1], rate_load, v_loads[0], k_loads[1], v_loads[1]]:
        load.start()

    piece = win // PIECES
    halo = [[
        pltpu.make_async_remote_copy(
            src_ref=src.at[pl.ds(rows - win + p * piece, piece)], dst_ref=dst.at[pl.ds(p * piece, piece)],
            send_sem=halo_send.at[i, p], recv_sem=halo_recv.at[i, p],
            device_id={"ctx": (me + 1) % n}, device_id_type=MESH,
        ) for p in range(PIECES)]
        for i, (src, dst) in enumerate(((k_hbm, kx), (v_hbm, vx)))
    ]

    def halo_start(i, p):
        @pl.when(me < n - 1)
        def _():
            halo[i][p].start()

    def meet():
        pl.semaphore_wait(barrier, n - 1 + len(peers))
        for p in range(PIECES):
            halo_start(0, p)

    @pl.when(me == 0)
    def _():
        kx[0:win, :] = jnp.zeros((win, width), BF16)
        vx[0:win, :] = jnp.zeros((win, width), BF16)

    total = rows * n
    done = {"F": 0}

    def forward():
        i = done["F"]
        done["F"] += 1
        if i == 0:
            for load in [k_loads[0], w_loads[0], w_loads[1], rate_load, v_loads[0]]:
                load.wait()
            for b in range(2, blocks):
                k_loads[b].start()
                v_loads[b].start()
            w_loads[2].start()
        else:
            k_loads[i].wait()
            v_loads[i].wait()
        if i == blocks - 1:
            for load in doc_loads + [q_load] + mom_loads + [gain_load]:
                load.start()
        at = block_at(i)
        kb = kx[block_at(i, win), :]
        h1 = jnp.dot(kb, w[0], preferred_element_type=F32)
        h3 = jnp.dot(kb, w[1], preferred_element_type=F32)
        vb = vx[block_at(i, win), :].astype(F32)
        rate = as_column(rates[:, at])[:, :1]
        u[at, :] = (rate * vb * (-1.0 / math.sqrt(total))).astype(BF16)
        sig = 1.0 / (1.0 + jnp.exp(-h1))
        act = h1 * sig
        dh[2, at, :] = (act * h3).astype(BF16)
        hold[0, at, :] = h3 * sig * (1.0 + h1 * (1.0 - sig))
        hold[1, at, :] = act

    def slot(c, j):
        return pl.ds((c % SPLIT) * crows + crows - (crows >> j), crows >> (j + 1))

    def scatter(c, j):
        return pltpu.make_async_remote_copy(
            src_ref=sbuf.at[c // SPLIT, slot(c, j), :], dst_ref=rbuf.at[c // SPLIT, slot(c, j), :],
            send_sem=rs_send.at[c, j], recv_sem=rs_recv.at[c, j],
            device_id={"ctx": partner[c][j]}, device_id_type=MESH)

    def scatter_start(c, j):
        half = crows >> (j + 1)
        sbuf[c // SPLIT, slot(c, j), :] = acc[c // SPLIT, at_rows(drop[c][j], half), :].astype(BF16)
        scatter(c, j).start()

    def scatter_finish(c, j):
        half = crows >> (j + 1)
        scatter(c, j).wait_recv()
        mine = at_rows(keep[c][j], half)
        acc[c // SPLIT, mine, :] = acc[c // SPLIT, mine, :] + rbuf[c // SPLIT, slot(c, j), :].astype(F32)

    def gather(c, j):
        mine = at_rows(keep[c][j], crows >> (j + 1))
        return pltpu.make_async_remote_copy(
            src_ref=cand.at[c // SPLIT, mine, :], dst_ref=cand.at[c // SPLIT, mine, :],
            send_sem=ag_send.at[c, j], recv_sem=ag_recv.at[c, j],
            device_id={"ctx": partner[c][j]}, device_id_type=MESH)

    def gather_wait(c, j):
        theirs = at_rows(drop[c][j], crows >> (j + 1))
        pltpu.make_async_remote_copy(
            src_ref=cand.at[c // SPLIT, theirs, :], dst_ref=cand.at[c // SPLIT, theirs, :],
            send_sem=ag_send.at[c, j], recv_sem=ag_recv.at[c, j],
            device_id={"ctx": partner[c][j]}, device_id_type=MESH).wait_recv()

    def doc_setup():
        for load in doc_loads:
            load.wait()
        doc_cols[...] = as_column(doc_row()[:, win:])

    def doc_row():
        pick = lax.broadcasted_iota(jnp.int32, docs.shape, 0) == seq
        return jnp.sum(jnp.where(pick, docs[...], 0), axis=0, keepdims=True).astype(F32)

    def attend(i):
        at = block_at(i)
        span = win + BLOCK
        kb = kx[pl.ds(i * BLOCK, span), :]
        scores = lax.dot_general(
            q[at, :], kb, (((1,), (1,)), ((), ())), preferred_element_type=F32
        ) * (1.0 / math.sqrt(width))
        qpos = lax.broadcasted_iota(jnp.int32, scores.shape, 0) + win
        kpos = lax.broadcasted_iota(jnp.int32, scores.shape, 1)
        first = win - offset - i * BLOCK
        valid = (
            (kpos <= qpos) & (kpos > qpos - win) & (kpos >= first)
            & (doc_row()[:, i * BLOCK:i * BLOCK + span] == doc_cols[at, :][:, :1])
        )
        scores = jnp.where(valid, scores, -1e30)
        top = jnp.max(scores, axis=1, keepdims=True)
        expo = jnp.exp(scores - top)
        norm = 1.0 / jnp.sum(expo, axis=1, keepdims=True)
        probs = expo.astype(BF16)
        here = max(win - i * BLOCK, 0)
        y[at, :] = jnp.dot(
            probs[:, here:], vx[pl.ds(i * BLOCK + here, span - here), :],
            preferred_element_type=F32) * norm
        if here:
            held[i, :, 0:here] = probs[:, 0:here]
            norms[i] = jnp.broadcast_to(norm, norms.shape[1:])

    def rest(i):
        at = block_at(i)
        here = win - i * BLOCK

        @pl.when(me > 0)
        def _():
            for p in range(PIECES):
                if p * piece >= i * BLOCK and p not in arrived:
                    halo[1][p].wait_recv()
                    arrived.append(p)
        y[at, :] = y[at, :] + jnp.dot(
            held[i, :, 0:here], vx[pl.ds(i * BLOCK, here), :],
            preferred_element_type=F32) * norms[i][:, :1]

    def keys_wait():
        @pl.when(me > 0)
        def _():
            for p in range(PIECES):
                halo[0][p].wait_recv()

    def prepare(c):
        mom_loads[c].wait()
        old = jnp.transpose(w[c // SPLIT, :, lanes_own[c]].astype(F32), (1, 0))
        base[c] = old - 0.9 * jnp.transpose(mom[c], (1, 0))
        rms = jnp.sqrt(jnp.mean(old * old, axis=1, keepdims=True) + 1e-06)
        old_rms[c] = jnp.broadcast_to(rms, old_rms.shape[1:])

    def renew(c):
        mine = at_rows(low[c], own)
        part = base[c, within[c], :] - acc[c // SPLIT, mine, :]
        ratio = old_rms[c, within[c], :][:, :1] * lax.rsqrt(
            jnp.mean(part * part, axis=1, keepdims=True) + 1e-06)
        cand[c // SPLIT, mine, :] = (part * ratio).astype(BF16)

    taken = [0] * chunks

    def advance(c):
        step = taken[c]
        if step == 2 * phases:
            return
        taken[c] += 1
        if step < phases:
            scatter_finish(c, step)
            if step + 1 < phases:
                scatter_start(c, step + 1)
            else:
                renew(c)
                gather(c, phases - 1).start()
        else:
            j = 2 * phases - 1 - step
            gather_wait(c, j)
            if j > 0:
                gather(c, j - 1).start()

    def finish(c, upto):
        while taken[c] < upto:
            advance(c)

    across = (((0,), (0,)), ((), ()))
    nt = (((1,), (1,)), ((), ()))

    def hcols(h):
        return pl.ds(h * crows, crows)

    def gradient(c):
        right = u[...] if c // SPLIT == 2 else kx[pl.ds(win, rows), :]
        cols = hcols(c % SPLIT)
        acc[c // SPLIT, cols, :] = lax.dot_general(
            dh[c // SPLIT, :, cols], right, across, preferred_element_type=F32)
        scatter_start(c, 0)

    def back(h):
        if h == 0:
            w_loads[2].wait()
        cols = hcols(h)
        for i in range(0, rows, QBLOCK):
            at = pl.ds(i, QBLOCK)
            dg = jnp.dot(u[at, :], w[2, :, cols], preferred_element_type=F32)
            dh[0, at, cols] = (dg * hold[0, at, cols]).astype(BF16)
            dh[1, at, cols] = (dg * hold[1, at, cols]).astype(BF16)

    def gate(h):
        finish(h, 2 * phases)
        cols = hcols(h)
        for i in range(0, rows, QBLOCK):
            at = pl.ds(i, QBLOCK)
            o1 = lax.dot_general(q[at, :], cand[0, cols, :], nt, preferred_element_type=F32)
            hold[0, at, cols] = o1 / (1.0 + jnp.exp(-o1))

    def mix(h):
        finish(SPLIT + h, 2 * phases)
        cols = hcols(h)
        for i in range(0, rows, QBLOCK):
            at = pl.ds(i, QBLOCK)
            o3 = lax.dot_general(q[at, :], cand[1, cols, :], nt, preferred_element_type=F32)
            gq[at, cols] = (hold[0, at, cols] * o3).astype(BF16)

    def product(at, h):
        return jnp.dot(gq[at, hcols(h)], cand[2, hcols(h), :], preferred_element_type=F32)

    def down(h):
        finish(2 * SPLIT + h, 2 * phases)
        for i in range(0, rows, QBLOCK):
            at = pl.ds(i, QBLOCK)
            y[at, :] = y[at, :] + product(at, h)

    def turn(c):
        wt[c] = jnp.transpose(cand[c], (1, 0))

    early = [i for i in range(blocks) if i * BLOCK >= win]
    late = [i for i in range(blocks) if i * BLOCK < win][::-1]
    final = early + late
    rests = list(late)
    steps = {
        "F": forward, "|": meet, "K": keys_wait, "D": doc_setup, "Q": q_load.wait,
        "E": lambda: attend(early.pop(0)), "S": lambda: attend(late.pop(0)),
        "r": lambda: rest(rests.pop(0)),
        "V": lambda: halo_start(1, pieces.pop(0)),
    }
    pieces = list(range(PIECES))[::-1]
    arrived = []
    for c in range(chunks):
        steps[f"g{c}"] = functools.partial(gradient, c)
        steps[f"P{c}"] = functools.partial(prepare, c)
        steps[f"{c}"] = functools.partial(advance, c)
    for h in range(SPLIT):
        steps[f"B{h}"] = functools.partial(back, h)
        steps[f"O{h}"] = functools.partial(gate, h)
        steps[f"M{h}"] = functools.partial(mix, h)
        steps[f"W{h}"] = functools.partial(down, h)
    for num, step in enumerate(PLAN):
        with jax.named_scope(f"st{num:02d}_{step}"):
            steps[step]()

    def squares_copy(d, i):
        return pltpu.make_async_remote_copy(
            src_ref=ss_own.at[i], dst_ref=ss_got.at[d, i],
            send_sem=ss_send.at[d, i], recv_sem=ss_recv.at[d, i],
            device_id={"hs": peers[d]}, device_id_type=MESH)

    with jax.named_scope("last"):
        finish(chunks - 1, 2 * phases)
    for i in final:
        with jax.named_scope(f"fwb{i}"):
            at = block_at(i)
            mixed = y[at, :] + product(at, SPLIT - 1)
            y[at, :] = mixed
            sq = mixed * mixed
            lanes = sq[:, 0:128]
            for s in range(1, width // 128):
                lanes = lanes + sq[:, s * 128:(s + 1) * 128]
            row = jnp.sum(jnp.transpose(lanes, (1, 0)), axis=0, keepdims=True)
            ss_own[i] = jnp.broadcast_to(row, ss_own.shape[1:])
            for d in range(len(peers)):
                squares_copy(d, i).start()
    with jax.named_scope("turn2"):
        for c in range(3):
            turn(c)
    with jax.named_scope("sends"):
        gain_load.wait()
        for c in range(chunks):
            for j in range(phases):
                scatter(c, j).wait_send()
                gather(c, j).wait_send()

        @pl.when(me < n - 1)
        def _():
            for i in range(2):
                for p in range(PIECES):
                    halo[i][p].wait_send()

    for i in final:
        with jax.named_scope(f"ss{i}"):
            part = ss_own[i]
            for d in range(len(peers)):
                squares_copy(d, i).wait_recv()
                part = part + ss_got[d, i]
            ss_out[i] = part
            for d in range(len(peers)):
                squares_copy(d, i).wait_send()


def finale(count, y, ss, gain_ref, wt, out_hbm, new_hbm, outbuf, out_sem):
    rows, width = y.shape
    blocks = rows // BLOCK
    moves = [pltpu.make_async_copy(wt.at[c], new_hbm.at[c], out_sem.at[c]) for c in range(3)]
    for i in range(blocks):
        at = pl.ds(i * BLOCK, BLOCK)
        moves.append(pltpu.make_async_copy(outbuf.at[at], out_hbm.at[at], out_sem.at[3 + i]))
    for c in range(3):
        moves[c].start()
    gain = gain_ref[...]
    for i in range(blocks):
        at = pl.ds(i * BLOCK, BLOCK)
        scale = lax.rsqrt(as_column(ss[i][0:1, :]) * (1.0 / count) + 1e-06)
        for s in range(width // 128):
            cols = slice(s * 128, (s + 1) * 128)
            outbuf[at, cols] = (y[at, cols] * scale * gain[:, cols]).astype(BF16)
        moves[3 + i].start()
    for move in moves:
        move.wait()


def per_device(n, hs_count, queries, keys, values, rates, doc_ids, fast_weights, momentum, head_gain):
    rows, width = queries.shape[1:]
    _, mats, wrows, wcols = fast_weights.shape
    seqs = doc_ids.shape[0]
    heads = hs_count // seqs
    phases = n.bit_length() - 1
    blocks = rows // BLOCK
    ext = rows + WINDOW_TOKENS
    others = max(heads - 1, 1)
    any_spec = pl.BlockSpec(memory_space=pl.ANY)
    vmem = pl.BlockSpec(memory_space=pltpu.VMEM)
    dma = pltpu.SemaphoreType.DMA
    mixed, turned, squares, gain = pl.pallas_call(
        functools.partial(kernel, n, heads, seqs),
        out_shape=(
            pltpu.VMEM((rows, width), F32),
            pltpu.VMEM((mats, wrows, wcols), BF16),
            pltpu.VMEM((blocks, 8, BLOCK), F32),
            pltpu.VMEM((1, width), F32),
        ),
        in_specs=[any_spec] * 8,
        out_specs=(vmem,) * 4,
        scratch_shapes=[
            pltpu.VMEM((rows, width), BF16),
            pltpu.VMEM((ext, width), BF16),
            pltpu.VMEM((ext, width), BF16),
            pltpu.VMEM((mats, wrows, wcols), BF16),
            pltpu.VMEM((SPLIT * mats, wrows, 128), F32),
            pltpu.VMEM((seqs, ext), jnp.int32),
            pltpu.VMEM((1, rows), F32),
            pltpu.VMEM((mats, rows, wcols), BF16),
            pltpu.VMEM((rows, width), BF16),
            pltpu.VMEM((mats, wrows, wcols), F32),
            pltpu.VMEM((mats, wrows, wcols), BF16),
            pltpu.VMEM((mats, wrows, wcols), BF16),
            pltpu.VMEM((mats, wrows, wcols), BF16),
            pltpu.VMEM((SPLIT * mats, 128, wrows), F32),
            pltpu.VMEM((SPLIT * mats, 128, 128), F32),
            pltpu.VMEM((2, rows, wcols), F32),
            pltpu.VMEM((rows, wcols), BF16),
            pltpu.VMEM((WINDOW_TOKENS // BLOCK, BLOCK, WINDOW_TOKENS), BF16),
            pltpu.VMEM((WINDOW_TOKENS // BLOCK, BLOCK, 128), F32),
            pltpu.VMEM((blocks, 8, BLOCK), F32),
            pltpu.VMEM((others, blocks, 8, BLOCK), F32),
            pltpu.VMEM((rows, 128), F32),
            dma((blocks,)), dma((blocks,)), dma((3,)), dma((5 + SPLIT * mats,)), dma((2, PIECES)), dma((2, PIECES)),
            dma((SPLIT * mats, phases)), dma((SPLIT * mats, phases)),
            dma((SPLIT * mats, phases)), dma((SPLIT * mats, phases)),
            dma((others, blocks)), dma((others, blocks)),
        ],
        compiler_params=pltpu.CompilerParams(
            collective_id=0, has_side_effects=True, vmem_limit_bytes=48 * 1024 * 1024),
        name="lact_block",
    )(*[pltpu.with_memory_space_constraint(x, pltpu.HBM) for x in (
        queries[0], keys[0], values[0], rates, doc_ids, fast_weights[0], momentum[0], head_gain)])
    out, fresh = pl.pallas_call(
        functools.partial(finale, heads * width),
        out_shape=(
            jax.ShapeDtypeStruct((rows, width), BF16),
            jax.ShapeDtypeStruct((mats, wrows, wcols), BF16),
        ),
        in_specs=[vmem] * 4,
        out_specs=(any_spec, any_spec),
        scratch_shapes=[pltpu.VMEM((rows, width), BF16), dma((3 + blocks,))],
        compiler_params=pltpu.CompilerParams(vmem_limit_bytes=16 * 1024 * 1024),
        name="lact_finish",
    )(mixed, squares, gain, turned)
    return out[None], fresh[None]


def solution(mesh):
    return jax.shard_map(
        functools.partial(per_device, mesh.shape["ctx"], mesh.shape["hs"]),
        mesh=mesh,
        in_specs=(
            P("hs", "ctx", None),
            P("hs", "ctx", None),
            P("hs", "ctx", None),
            P("hs", "ctx"),
            P(),
            P("hs", None, None, None),
            P("hs", None, None, None),
            P("hs", None),
        ),
        out_specs=(P("hs", "ctx", None), P("hs", None, None, None)),
        check_vma=False,
    )
```

time: 44.1 us -> 40.9 us (0.927)
  local copies, waits for them, and re-layouts: 3.64 us -> 0 us
  Pallas kernels: 39.6 us -> 40.1 us
    unnamed x4 -> x0, local copies, waits for them, and re-layouts: 3.64 us -> none
    pallas_call x1 -> x2, Pallas kernels: 39.6 us -> 40.1 us  [the longest x1 38.5 us: per_device(): pl.pallas_call(functools.partial(kernel, n, heads, seqs), out_shape=(pltp...]
where the time goes in v1:
time: 40.9 us; the launch traced here: 40.7 us
  Pallas kernels  40.1 us (98%)
  between operations  0.64 us (2%)
    pallas_call x1, Pallas kernels, per_device(): pl.pallas_call(functools.partial(kernel, n, heads, seqs), out_shape=(pltp...  38.5 us
    pallas_call x1, Pallas kernels, per_device(): pl.pallas_call(functools.partial(finale, heads * width), out_shape=(jax.S...  1.54 us

profile of v1, /device:TPU:0, one launch (start us, length us, event | category | flops | bytes accessed | tf_op | source)
XLA Modules:
  0.0 40.7 jit_solution(3664422555953366961)
XLA Ops:
  0.6 38.5 %lact_block.1 = (f32[1024,512]{1,0:T(8,128)S(1)}, bf16[3,512,512]{2,1,0:T(8,128)(2,1)S(1)}, f32[4,8,256]{2,1,0:T(8,128)S(1)}, f32[1,512]{1,0:T(1,128)S(1)}) custom-call(bf16[1024,512]{1,0:T(8,128)(2,1)} %bitcast.9, bf16[1024,512]{1,0:T(8,128)(2,1)} %bitcast.10, bf16[1024,512]{1,0:T(8,128)(2,1)} %bitcast.11, f32[1,1024]{1,0:T(1,128)} %rates_hbm.1, ...), custom_call_target="tpu_custom_call" | custom-call | tf_op jit(solution)/shard_map/lact_block/pallas_call | solution.py:458
  39.2 1.5 %lact_finish.1 = (bf16[1024,512]{1,0:T(8,128)(2,1)}, bf16[3,512,512]{2,1,0:T(8,128)(2,1)}) custom-call(f32[1024,512]{1,0:T(8,128)S(1)} %get-tuple-element.8.y, f32[4,8,256]{2,1,0:T(8,128)S(1)} %get-tuple-element.9.ss, f32[1,512]{1,0:T(1,128)S(1)} %get-tuple-element.10.gain_ref, bf16[3,512,512]{2,1,0:T(8,128)(2,1)S(1)} %get-tuple-element.11.wt), custom_call_target="tpu_custom_call" | custom-call | tf_op jit(solution)/shard_map/lact_finish/pallas_call | solution.py:501
